TPU v7x, 32 devices: a whole 2x2x4 slice. The times are simulated.
32 devices in a mesh: strip: 8 (over y, x, core), mode: 4 (over z).
Axes of the slice: x: 2, y: 2, z: 4, core: 2. Of those that a mesh axis runs over, the one named last changes fastest.
Arguments:
- object_field: float32 [2, 2048, 384], P(None, 'strip'), may hold values from -5 to 5
- probe_modes: float32 [2, 8, 256, 256], P(None, 'mode'), may hold values from -2.5 to 2.5
- measured: float32 [8, 4, 256, 256], P('strip'), may hold values from 0.1 to 27
- positions: int32 [8, 4, 2], P('strip'), may hold values from 0 to 128, as said below
Outputs:
- object_new: float32 [2, 2048, 384], P(None, 'strip')
Inputs may be any that keep to these rules, and one draw needn't show every extreme that they name: positions[s,k,0] is the first row of window k within strip s and positions[s,k,1] its first column; the windows of every strip form a two by two raster with small offsets: windows 0 and 3 start at row 128, windows 1 and 2 at row 0, window 1 at column 128, window 3 at most 16 columns left of it, windows 0 and 2 at columns 0 to 16.
All inputs are finite; a program needn't handle non-finite values.
Results may differ from a plain program's by a relative error of at most 0.0001.
Values sent between devices are 32-bit elements; how exact they have to be, the bound alone decides.
A program may use at most 128 MiB of HBM per device.

v0:
```python
import jax
import jax.numpy as jnp
from jax import lax
from jax.sharding import PartitionSpec as P

HALO = 128
ITERS = 3
regularizer = 0.1
step_scale = 0.3
epsilon = 1e-06
highest = lax.Precision.HIGHEST


def from_behind(block, axis, distance):
    devices = range(lax.axis_size(axis))
    route = [(i - distance, i) for i in devices if i - distance in devices]
    return lax.ppermute(block, axis, route)


def dft_tables(length):
    indices = jnp.arange(length, dtype=jnp.int32)
    phases = indices[:, None] * indices[None, :] % length
    angles = phases.astype(jnp.float32) * (2.0 * jnp.pi / length)
    scaling = 1.0 / jnp.sqrt(jnp.float32(length))
    return (jnp.cos(angles) * scaling, -jnp.sin(angles) * scaling)


def transform(part_real, part_imag, cosine_table, sine_table):
    length = cosine_table.shape[0]
    stacked_rows = jnp.concatenate([cosine_table, sine_table], axis=0)
    left_real = jnp.einsum("jk,bkl->bjl", stacked_rows, part_real, precision=highest)
    left_imag = jnp.einsum("jk,bkl->bjl", stacked_rows, part_imag, precision=highest)
    middle_real = left_real[:, :length] - left_imag[:, length:]
    middle_imag = left_imag[:, :length] + left_real[:, length:]
    stacked_cols = jnp.concatenate([cosine_table, sine_table], axis=1)
    right_real = jnp.einsum("bjk,kl->bjl", middle_real, stacked_cols, precision=highest)
    right_imag = jnp.einsum("bjk,kl->bjl", middle_imag, stacked_cols, precision=highest)
    return (
        right_real[..., :length] - right_imag[..., length:],
        right_imag[..., :length] + right_real[..., length:],
    )


def body(object_field, probe_modes, measured, positions):
    stripe_rows = object_field.shape[1]
    width_cols = object_field.shape[2]
    window = probe_modes.shape[2]
    local_modes = probe_modes.shape[1]
    slots = positions.shape[1]
    halo_rows = HALO
    cosine_table, sine_table = dft_tables(window)
    rows_at = positions[0, :, 0]
    cols_at = positions[0, :, 1]
    total_cells = stripe_rows * lax.axis_size("strip") * width_cols
    measured_intensity = measured[0]
    probe_real = probe_modes[0][None]
    probe_imag = probe_modes[1][None]
    zero_index = jnp.zeros((), jnp.int32)
    for iteration in range(ITERS):
        below = from_behind(object_field[:, :halo_rows], "strip", -1)
        frame = jnp.concatenate([object_field, below], axis=1)
        patches = jnp.stack(
            [
                lax.dynamic_slice(
                    frame, (zero_index, rows_at[slot], cols_at[slot]), (2, window, window)
                )
                for slot in range(slots)
            ],
            axis=1,
        )
        patch_real = patches[0][:, None]
        patch_imag = patches[1][:, None]
        exit_real = probe_real * patch_real - probe_imag * patch_imag
        exit_imag = probe_real * patch_imag + probe_imag * patch_real
        far_real, far_imag = transform(
            exit_real.reshape(-1, window, window),
            exit_imag.reshape(-1, window, window),
            cosine_table,
            sine_table,
        )
        far_real = far_real.reshape(slots, local_modes, window, window)
        far_imag = far_imag.reshape(slots, local_modes, window, window)
        probe_power = jnp.sum(far_real * far_real + far_imag * far_imag, axis=1)
        summed_power = lax.psum(probe_power, "mode")
        object_update = (
            jnp.sqrt((measured_intensity + regularizer) / (summed_power + regularizer)) - 1.0
        )
        shift_real = (object_update[:, None] * far_real).reshape(-1, window, window)
        shift_imag = (object_update[:, None] * far_imag).reshape(-1, window, window)
        delta_real, delta_imag = transform(shift_real, shift_imag, cosine_table, -sine_table)
        delta_real = delta_real.reshape(slots, local_modes, window, window)
        delta_imag = delta_imag.reshape(slots, local_modes, window, window)
        grad_real = jnp.sum(probe_real * delta_real + probe_imag * delta_imag, axis=1)
        grad_imag = jnp.sum(probe_real * delta_imag - probe_imag * delta_real, axis=1)
        grad_real, grad_imag = lax.psum((grad_real, grad_imag), "mode")
        frame_grad = jnp.zeros((2, stripe_rows + halo_rows, width_cols), jnp.float32)
        for slot in range(slots):
            start = (zero_index, rows_at[slot], cols_at[slot])
            current = lax.dynamic_slice(frame_grad, start, (2, window, window))
            frame_grad = lax.dynamic_update_slice(
                frame_grad, current + jnp.stack([grad_real[slot], grad_imag[slot]]), start
            )
        arrived = from_behind(frame_grad[:, stripe_rows:], "strip", 1)
        gradient = jnp.concatenate(
            [frame_grad[:, :halo_rows] + arrived, frame_grad[:, halo_rows:stripe_rows]], axis=1
        )
        square_sum = lax.psum(jnp.sum(gradient * gradient), "strip")
        step_factor = step_scale / jnp.sqrt(square_sum / total_cells + epsilon)
        object_field = object_field + step_factor * gradient
    return object_field


def solution(mesh):
    return jax.shard_map(
        body,
        mesh=mesh,
        in_specs=(
            P(None, "strip", None),
            P(None, "mode", None, None),
            P("strip", None, None, None),
            P("strip", None, None),
        ),
        out_specs=P(None, "strip", None),
        check_vma=False,
    )
```

profile of v0, /device:TPU:4, one launch (start us, length us, event | category | flops | bytes accessed | tf_op | source)
XLA Modules:
  0.0 812.3 jit_solution(13496103538297187486)
XLA Ops:
  31.6 7.1 convolution_bitcast_fusion.10
  38.7 7.5 convolution_bitcast_fusion.11
  46.3 3.7 fusion.22
  50.0 3.7 fusion.20
  58.5 51.5 %all-reduce.10.cloned.1.call-done = f32[4,256,256]{2,1,0:T(8,128)} async-done(((f32[4,256,256]{2,1,0:T(8,128)}), f32[4,256,256]{2,1,0:T(8,128)}) %all-reduce.10.cloned.1.call-update) | async-done | bytes 1048592 | tf_op jit(solution)/shard_map/psum | solution.py:84
  111.6 4.1 bitcast_multiply_fusion.5
  115.7 7.2 convolution_bitcast_fusion.9
  122.9 7.6 convolution_bitcast_fusion.8
  134.2 3.7 fusion.18
  140.1 85.5 %all-reduce.20.cloned.1.call-done = (f32[4,256,256]{2,1,0:T(8,128)}, f32[4,256,256]{2,1,0:T(8,128)}) async-done(((f32[4,256,256]{2,1,0:T(8,128)}, f32[4,256,256]{2,1,0:T(8,128)}), (f32[4,256,256]{2,1,0:T(8,128)}, f32[4,256,256]{2,1,0:T(8,128)})) %all-reduce.20.cloned.1.call-update) | async-done | bytes 2097168 | tf_op jit(solution)/shard_map/psum | solution.py:95
  228.8 6.6 dynamic_update_slice.36
  236.6 5.3 dynamic_update_slice.37
  243.2 8.1 dynamic_update_slice.38
  252.5 6.6 dynamic_update_slice.39
  261.1 8.1 collective-permute-done.1
  270.8 12.5 %psum.87 = f32[]{:T(128)} all-reduce(f32[]{:T(128)} %multiply_reduce_fusion.2), channel_id=1, replica_groups=mesh['strip'=8,'mode'=4] {'strip'}, use_global_device_ids=true, to_apply=%region_7.8 | all-reduce | flops 1 | bytes 8 | tf_op jit(solution)/shard_map/psum | solution.py:107
  287.4 5.1 collective-permute-done.2
  294.6 7.1 convolution_bitcast_fusion.6
  301.7 7.3 convolution_bitcast_fusion.7
  309.0 3.7 fusion.14
  312.8 3.7 fusion.12
  320.6 51.1 %all-reduce.12.cloned.1.call-done = f32[4,256,256]{2,1,0:T(8,128)} async-done(((f32[4,256,256]{2,1,0:T(8,128)}), f32[4,256,256]{2,1,0:T(8,128)}) %all-reduce.12.cloned.1.call-update) | async-done | bytes 1048592 | tf_op jit(solution)/shard_map/psum | solution.py:84
  373.3 4.1 bitcast_multiply_fusion.3
  377.4 7.2 convolution_bitcast_fusion.5
  384.6 7.4 convolution_bitcast_fusion.4
  401.5 85.5 %all-reduce.18.cloned.1.call-done = (f32[4,256,256]{2,1,0:T(8,128)}, f32[4,256,256]{2,1,0:T(8,128)}) async-done(((f32[4,256,256]{2,1,0:T(8,128)}, f32[4,256,256]{2,1,0:T(8,128)}), (f32[4,256,256]{2,1,0:T(8,128)}, f32[4,256,256]{2,1,0:T(8,128)})) %all-reduce.18.cloned.1.call-update) | async-done | bytes 2097168 | tf_op jit(solution)/shard_map/psum | solution.py:95
  490.2 6.6 dynamic_update_slice.40
  498.0 5.3 dynamic_update_slice.41
  504.6 8.1 dynamic_update_slice.42
  513.9 6.6 dynamic_update_slice.43
  522.5 8.1 collective-permute-done.3
  532.2 12.5 %psum.91 = f32[]{:T(128)} all-reduce(f32[]{:T(128)} %multiply_reduce_fusion.1), channel_id=1, replica_groups=mesh['strip'=8,'mode'=4] {'strip'}, use_global_device_ids=true, to_apply=%region_15.16 | all-reduce | flops 1 | bytes 8 | tf_op jit(solution)/shard_map/psum | solution.py:107
  549.1 4.9 collective-permute-done.4
  556.1 7.1 convolution_bitcast_fusion.2
  563.1 7.2 convolution_bitcast_fusion.3
  570.4 3.7 fusion.6
  574.1 3.7 fusion.4
  581.7 51.3 %all-reduce.14.cloned.1.call-done = f32[4,256,256]{2,1,0:T(8,128)} async-done(((f32[4,256,256]{2,1,0:T(8,128)}), f32[4,256,256]{2,1,0:T(8,128)}) %all-reduce.14.cloned.1.call-update) | async-done | bytes 1048592 | tf_op jit(solution)/shard_map/psum | solution.py:84
  634.9 4.1 bitcast_multiply_fusion.1
  639.0 7.2 convolution_bitcast_fusion.1
  646.2 7.6 convolution_bitcast_fusion
  663.3 85.6 %all-reduce.16.cloned.1.call-done = (f32[4,256,256]{2,1,0:T(8,128)}, f32[4,256,256]{2,1,0:T(8,128)}) async-done(((f32[4,256,256]{2,1,0:T(8,128)}, f32[4,256,256]{2,1,0:T(8,128)}), (f32[4,256,256]{2,1,0:T(8,128)}, f32[4,256,256]{2,1,0:T(8,128)})) %all-reduce.16.cloned.1.call-update) | async-done | bytes 2097168 | tf_op jit(solution)/shard_map/psum | solution.py:95
  751.9 6.8 dynamic_update_slice.44
  759.9 5.3 dynamic_update_slice.45
  765.4 8.1 dynamic_update_slice.46
  773.7 6.6 dynamic_update_slice.47
  782.2 8.1 collective-permute-done.5
  791.2 12.5 %psum.95 = f32[]{:T(128)} all-reduce(f32[]{:T(128)} %multiply_reduce_fusion), channel_id=1, replica_groups=mesh['strip'=8,'mode'=4] {'strip'}, use_global_device_ids=true, to_apply=%region_23.24 | all-reduce | flops 1 | bytes 8 | tf_op jit(solution)/shard_map/psum | solution.py:107
  (117 shorter events, 93.3 us)
Async XLA Ops:
  6.5 23.4 %copy-start.11 = (f32[2,2,256,256]{3,2,1,0:T(8,128)S(1)}, f32[2,2,256,256]{3,2,1,0:T(8,128)}, u32[]{:S(2)}) copy-start(f32[2,2,256,256]{3,2,1,0:T(8,128)} %param.5) | copy-start | bytes 3145732
  6.5 103.5 %all-reduce.10.cloned.1.call-start = ((), (), s32[]{:S(2)}) async-start(), calls=%async_computation | async-start | bytes 2097152 | tf_op jit(solution)/shard_map/psum | solution.py:84
  8.4 21.7 %collective-permute-start = (f32[2,128,384]{2,1,0:T(8,128)}, f32[2,128,384]{2,1,0:T(8,128)S(1)}, u32[]{:S(2)}, u32[]{:S(2)}) collective-permute-start(f32[2,128,384]{2,1,0:T(8,128)} %slice.359), channel_id=1, source_target_pairs={{4,0},{8,4},{12,8},{16,12},{20,16},{24,20},{28,24},{5,1},{9,5},{13... | collective-permute-start | bytes 1179656 | tf_op jit(solution)/shard_map/ppermute | solution.py:17
  50.0 3.7 copy-start
  53.7 1.9 copy-start.1
  55.7 54.3 %copy-start.7 = (f32[1,4,256,256]{3,2,1,0:T(8,128)S(1)}, f32[1,4,256,256]{3,2,1,0:T(8,128)}, u32[]{:S(2)}) copy-start(f32[1,4,256,256]{3,2,1,0:T(8,128)} %param.6) | copy-start | bytes 3145732
  57.4 168.2 %all-reduce.20.cloned.1.call-start = ((), (), s32[]{:S(2)}) async-start(), calls=%async_computation.5 | async-start | bytes 4194304 | tf_op jit(solution)/shard_map/psum | solution.py:95
  140.0 231.6 %all-reduce.12.cloned.1.call-start = ((), (), s32[]{:S(2)}) async-start(), calls=%async_computation.1 | async-start | bytes 2097152 | tf_op jit(solution)/shard_map/psum | solution.py:84
  225.6 2.2 copy-start.12
  259.1 10.0 %collective-permute-start.1 = (f32[2,128,384]{2,1,0:T(8,128)S(1)}, f32[2,128,384]{2,1,0:T(8,128)S(1)}, u32[]{:S(2)}, u32[]{:S(2)}) collective-permute-start(f32[2,128,384]{2,1,0:T(8,128)S(1)} %slice.485), channel_id=1, source_target_pairs={{0,4},{4,8},{8,12},{12,16},{16,20},{20,24},{24,28},{1,5},{5,9},{9,... | collective-permute-start | bytes 1179656 | tf_op jit(solution)/shard_map/ppermute | solution.py:17
  269.2 0.7 copy-start.10
  285.3 8.6 %copy-start.6 = (f32[2,256,384]{2,1,0:T(8,128)}, f32[2,256,384]{2,1,0:T(8,128)S(1)}, u32[]{:S(2)}) copy-start(f32[2,256,384]{2,1,0:T(8,128)S(1)} %multiply_add_fusion.8) | copy-start | bytes 2359300
  285.3 7.2 collective-permute-start.2
  312.7 3.7 copy-start.4
  316.5 1.9 copy-start.5
  318.4 53.2 %copy-start.8 = (f32[1,4,256,256]{3,2,1,0:T(8,128)S(1)}, f32[1,4,256,256]{3,2,1,0:T(8,128)}, u32[]{:S(2)}) copy-start(f32[1,4,256,256]{3,2,1,0:T(8,128)} %param.6) | copy-start | bytes 3145732
  320.0 167.0 %all-reduce.18.cloned.1.call-start = ((), (), s32[]{:S(2)}) async-start(), calls=%async_computation.4 | async-start | bytes 4194304 | tf_op jit(solution)/shard_map/psum | solution.py:95
  401.4 231.6 %all-reduce.14.cloned.1.call-start = ((), (), s32[]{:S(2)}) async-start(), calls=%async_computation.2 | async-start | bytes 2097152 | tf_op jit(solution)/shard_map/psum | solution.py:84
  487.0 2.2 copy-start.13
  520.5 10.0 %collective-permute-start.3 = (f32[2,128,384]{2,1,0:T(8,128)S(1)}, f32[2,128,384]{2,1,0:T(8,128)S(1)}, u32[]{:S(2)}, u32[]{:S(2)}) collective-permute-start(f32[2,128,384]{2,1,0:T(8,128)S(1)} %slice.515), channel_id=1, source_target_pairs={{0,4},{4,8},{8,12},{12,16},{16,20},{20,24},{24,28},{1,5},{5,9},{9,... | collective-permute-start | bytes 1179656 | tf_op jit(solution)/shard_map/ppermute | solution.py:17
  530.6 0.7 copy-start.9
  546.8 7.2 collective-permute-start.4
  574.1 3.7 copy-start.2
  577.8 1.9 copy-start.3
  581.4 167.5 %all-reduce.16.cloned.1.call-start = ((), (), s32[]{:S(2)}) async-start(), calls=%async_computation.3 | async-start | bytes 4194304 | tf_op jit(solution)/shard_map/psum | solution.py:95
  748.9 2.1 copy-start.14
  780.3 10.0 %collective-permute-start.5 = (f32[2,128,384]{2,1,0:T(8,128)S(1)}, f32[2,128,384]{2,1,0:T(8,128)S(1)}, u32[]{:S(2)}, u32[]{:S(2)}) collective-permute-start(f32[2,128,384]{2,1,0:T(8,128)S(1)} %slice.545), channel_id=1, source_target_pairs={{0,4},{4,8},{8,12},{12,16},{16,20},{20,24},{24,28},{1,5},{5,9},{9,... | collective-permute-start | bytes 1179656 | tf_op jit(solution)/shard_map/ppermute | solution.py:17
Sparse Core Ops, SparseCore 0:
  57.6 52.3 all-reduce.9
  140.1 85.4 all-reduce.19
  320.2 51.4 all-reduce.11
  401.5 85.4 all-reduce.17
  581.5 51.4 all-reduce.13
  663.4 85.4 all-reduce.15
where the time goes:
time: 822 us; the launch traced here: 812 us
  waiting for transfers between devices  445 us (54%)
  matrix products  132 us (16%)
  local copies, waits for them, and re-layouts  102 us (12%)
  other arithmetic  50.7 us (6%)
  blocking collectives  37.5 us (5%)
  between operations  31.3 us (4%)
  starting transfers between devices  13.8 us (2%)
    psum x3, waiting for transfers between devices, body(): grad_real, grad_imag = lax.psum((grad_real, grad_imag), 'mode')  257 us
    psum x3, waiting for transfers between devices, body(): summed_power = lax.psum(probe_power, 'mode')  154 us
    dynamic_update_slice x12, local copies, waits for them, and re-layouts, body(): lax.dynamic_update_slice(frame_grad, current + jnp.stack([grad_real[slot]...  79.7 us
    dot_general x6, matrix products, transform(): jnp.einsum('jk,bkl->bjl', stacked_rows, part_imag, precision=highest)  43.8 us
    dot_general x6, matrix products, transform(): jnp.einsum('jk,bkl->bjl', stacked_rows, part_real, precision=highest)  43.7 us
    psum x3, blocking collectives, body(): square_sum = lax.psum(jnp.sum(gradient * gradient), 'strip')  37.5 us
    ppermute x6, waiting for transfers between devices, from_behind(): return lax.ppermute(block, axis, route)  34.2 us
    dot_general x6, matrix products, transform(): jnp.einsum('bjk,kl->bjl', middle_real, stacked_cols, precision=highest)  22.2 us
  transfers between devices with their start and end apart: 12, of which 11 were waited for; matrix products, arithmetic and copies ran while one was open for 1% of the time, Pallas kernels for 0%

commit v1 on v0

--- a/solution.py
+++ b/solution.py
@@ -81,7 +81,13 @@
         far_real = far_real.reshape(slots, local_modes, window, window)
         far_imag = far_imag.reshape(slots, local_modes, window, window)
         probe_power = jnp.sum(far_real * far_real + far_imag * far_imag, axis=1)
-        summed_power = lax.psum(probe_power, "mode")
+        peers = lax.axis_size("mode")
+        summed_power, far = (probe_power, 1)
+        while far < peers:
+            summed_power = summed_power + lax.ppermute(
+                summed_power, "mode", [(i_2, i_2 ^ far) for i_2 in range(peers)]
+            )
+            far = 2 * far
         object_update = (
             jnp.sqrt((measured_intensity + regularizer) / (summed_power + regularizer)) - 1.0
         )

time: 822 us -> 865 us (1.052)
  waiting for transfers between devices: 445 us -> 503 us
  other arithmetic: 50.7 us -> 35.9 us
    ppermute x0 -> x6, waiting for transfers between devices: none -> 211 us  [body(): lax.ppermute(summed_power, 'mode', [(i_2, i_2 ^ far) for i_2 in range(pee...]
    psum x3 -> x0, waiting for transfers between devices: 154 us -> none  [body(): summed_power = lax.psum(probe_power, 'mode')]
    mul x3, other arithmetic: 12.3 us -> 2 us  [body(): shift_real = (object_update[:, None] * far_real).reshape(-1, window, window)]
  transfers between devices with their start and end apart: 12 -> 15, of which waited for: 11 -> 14; matrix products, arithmetic and copies ran while one was open for 1% -> 1% of each run, Pallas kernels for 0% -> 0%
where the time goes in v1:
time: 865 us; the launch traced here: 856 us
  waiting for transfers between devices  503 us (58%)
  matrix products  131 us (15%)
  local copies, waits for them, and re-layouts  96.7 us (11%)
  blocking collectives  37.4 us (4%)
  other arithmetic  35.9 us (4%)
  between operations  30.7 us (4%)
  starting transfers between devices  20.9 us (2%)
    psum x3, waiting for transfers between devices, body(): grad_real, grad_imag = lax.psum((grad_real, grad_imag), 'mode')  257 us
    ppermute x6, waiting for transfers between devices, body(): lax.ppermute(summed_power, 'mode', [(i_2, i_2 ^ far) for i_2 in range(pee...  211 us
    dynamic_update_slice x12, local copies, waits for them, and re-layouts, body(): lax.dynamic_update_slice(frame_grad, current + jnp.stack([grad_real[slot]...  79.8 us
    dot_general x6, matrix products, transform(): jnp.einsum('jk,bkl->bjl', stacked_rows, part_imag, precision=highest)  43.4 us
    dot_general x6, matrix products, transform(): jnp.einsum('jk,bkl->bjl', stacked_rows, part_real, precision=highest)  42.5 us
    psum x3, blocking collectives, body(): square_sum = lax.psum(jnp.sum(gradient * gradient), 'strip')  37.4 us
    ppermute x6, waiting for transfers between devices, from_behind(): return lax.ppermute(block, axis, route)  34.6 us
    dot_general x6, matrix products, transform(): jnp.einsum('bjk,kl->bjl', middle_imag, stacked_cols, precision=highest)  22.6 us
  transfers between devices with their start and end apart: 15, of which 14 were waited for; matrix products, arithmetic and copies ran while one was open for 1% of the time, Pallas kernels for 0%

profile of v1, /device:TPU:4, one launch (start us, length us, event | category | flops | bytes accessed | tf_op | source)
XLA Modules:
  0.0 855.8 jit_solution(6176502635704196094)
XLA Ops:
  31.4 7.0 convolution_bitcast_fusion.10
  38.3 6.9 convolution_bitcast_fusion.11
  45.2 3.8 fusion.22
  49.0 3.8 fusion.20
  55.4 23.1 %collective-permute-done.1 = f32[4,256,256]{2,1,0:T(8,128)S(1)} collective-permute-done((f32[4,256,256]{2,1,0:T(8,128)S(1)}, f32[4,256,256]{2,1,0:T(8,128)S(1)}, u32[]{:S(2)}, u32[]{:S(2)}) %collective-permute-start.1) | collective-permute-done | bytes 1048608 | tf_op jit(solution)/shard_map/ppermute | solution.py:87
  82.3 43.6 %collective-permute-done.2 = f32[4,256,256]{2,1,0:T(8,128)S(1)} collective-permute-done((f32[4,256,256]{2,1,0:T(8,128)S(1)}, f32[4,256,256]{2,1,0:T(8,128)S(1)}, u32[]{:S(2)}, u32[]{:S(2)}) %collective-permute-start.2) | collective-permute-done | bytes 1048608 | tf_op jit(solution)/shard_map/ppermute | solution.py:87
  127.1 7.2 convolution_bitcast_fusion.9
  134.3 7.7 convolution_bitcast_fusion.8
  142.0 3.7 fusion.16
  151.7 88.2 %all-reduce.11.cloned.1.call-done = (f32[4,256,256]{2,1,0:T(8,128)}, f32[4,256,256]{2,1,0:T(8,128)}) async-done(((f32[4,256,256]{2,1,0:T(8,128)}, f32[4,256,256]{2,1,0:T(8,128)}), (f32[4,256,256]{2,1,0:T(8,128)}, f32[4,256,256]{2,1,0:T(8,128)})) %all-reduce.11.cloned.1.call-update) | async-done | bytes 2097168 | tf_op jit(solution)/shard_map/psum | solution.py:101
  243.1 6.6 dynamic_update_slice.36
  251.0 5.3 dynamic_update_slice.37
  257.5 8.1 dynamic_update_slice.38
  266.8 6.6 dynamic_update_slice.39
  275.4 8.1 collective-permute-done.3
  285.1 12.5 %psum.65 = f32[]{:T(128)} all-reduce(f32[]{:T(128)} %multiply_reduce_fusion.2), channel_id=1, replica_groups=mesh['strip'=8,'mode'=4] {'strip'}, use_global_device_ids=true, to_apply=%region_6.7 | all-reduce | flops 1 | bytes 8 | tf_op jit(solution)/shard_map/psum | solution.py:113
  301.5 5.3 collective-permute-done.4
  309.0 7.0 convolution_bitcast_fusion.6
  316.0 7.1 convolution_bitcast_fusion.7
  323.1 3.8 fusion.14
  326.9 3.8 fusion.12
  331.9 24.9 %collective-permute-done.5 = f32[4,256,256]{2,1,0:T(8,128)S(1)} collective-permute-done((f32[4,256,256]{2,1,0:T(8,128)S(1)}, f32[4,256,256]{2,1,0:T(8,128)S(1)}, u32[]{:S(2)}, u32[]{:S(2)}) %collective-permute-start.5) | collective-permute-done | bytes 1048608 | tf_op jit(solution)/shard_map/ppermute | solution.py:87
  358.4 47.4 %collective-permute-done.6 = f32[4,256,256]{2,1,0:T(8,128)S(1)} collective-permute-done((f32[4,256,256]{2,1,0:T(8,128)S(1)}, f32[4,256,256]{2,1,0:T(8,128)S(1)}, u32[]{:S(2)}, u32[]{:S(2)}) %collective-permute-start.6) | collective-permute-done | bytes 1048608 | tf_op jit(solution)/shard_map/ppermute | solution.py:87
  407.1 7.2 convolution_bitcast_fusion.5
  414.3 7.6 convolution_bitcast_fusion.4
  431.5 84.5 %all-reduce.9.cloned.1.call-done = (f32[4,256,256]{2,1,0:T(8,128)}, f32[4,256,256]{2,1,0:T(8,128)}) async-done(((f32[4,256,256]{2,1,0:T(8,128)}, f32[4,256,256]{2,1,0:T(8,128)}), (f32[4,256,256]{2,1,0:T(8,128)}, f32[4,256,256]{2,1,0:T(8,128)})) %all-reduce.9.cloned.1.call-update) | async-done | bytes 2097168 | tf_op jit(solution)/shard_map/psum | solution.py:101
  519.2 6.6 dynamic_update_slice.40
  527.0 5.3 dynamic_update_slice.41
  533.6 8.1 dynamic_update_slice.42
  542.9 6.6 dynamic_update_slice.43
  551.4 8.1 collective-permute-done.7
  561.1 12.5 %psum.68 = f32[]{:T(128)} all-reduce(f32[]{:T(128)} %multiply_reduce_fusion.1), channel_id=1, replica_groups=mesh['strip'=8,'mode'=4] {'strip'}, use_global_device_ids=true, to_apply=%region_13.14 | all-reduce | flops 1 | bytes 8 | tf_op jit(solution)/shard_map/psum | solution.py:113
  577.7 5.1 collective-permute-done.8
  584.9 7.0 convolution_bitcast_fusion.2
  591.9 6.9 convolution_bitcast_fusion.3
  598.8 3.8 fusion.6
  602.7 3.8 fusion.4
  607.6 24.9 %collective-permute-done.9 = f32[4,256,256]{2,1,0:T(8,128)S(1)} collective-permute-done((f32[4,256,256]{2,1,0:T(8,128)S(1)}, f32[4,256,256]{2,1,0:T(8,128)S(1)}, u32[]{:S(2)}, u32[]{:S(2)}) %collective-permute-start.9) | collective-permute-done | bytes 1048608 | tf_op jit(solution)/shard_map/ppermute | solution.py:87
  634.2 47.4 %collective-permute-done.10 = f32[4,256,256]{2,1,0:T(8,128)S(1)} collective-permute-done((f32[4,256,256]{2,1,0:T(8,128)S(1)}, f32[4,256,256]{2,1,0:T(8,128)S(1)}, u32[]{:S(2)}, u32[]{:S(2)}) %collective-permute-start.10) | collective-permute-done | bytes 1048608 | tf_op jit(solution)/shard_map/ppermute | solution.py:87
  683.1 7.2 convolution_bitcast_fusion.1
  690.3 7.2 convolution_bitcast_fusion
  707.0 84.5 %all-reduce.7.cloned.1.call-done = (f32[4,256,256]{2,1,0:T(8,128)}, f32[4,256,256]{2,1,0:T(8,128)}) async-done(((f32[4,256,256]{2,1,0:T(8,128)}, f32[4,256,256]{2,1,0:T(8,128)}), (f32[4,256,256]{2,1,0:T(8,128)}, f32[4,256,256]{2,1,0:T(8,128)})) %all-reduce.7.cloned.1.call-update) | async-done | bytes 2097168 | tf_op jit(solution)/shard_map/psum | solution.py:101
  794.6 6.8 dynamic_update_slice.44
  802.6 5.3 dynamic_update_slice.45
  809.1 8.1 dynamic_update_slice.46
  817.4 6.6 dynamic_update_slice.47
  826.0 8.1 collective-permute-done.11
  834.9 12.5 %psum.71 = f32[]{:T(128)} all-reduce(f32[]{:T(128)} %multiply_reduce_fusion), channel_id=1, replica_groups=mesh['strip'=8,'mode'=4] {'strip'}, use_global_device_ids=true, to_apply=%region_20.21 | all-reduce | flops 1 | bytes 8 | tf_op jit(solution)/shard_map/psum | solution.py:113
  (113 shorter events, 92.1 us)
Async XLA Ops:
  6.5 23.2 %copy-start.6 = (f32[2,2,256,256]{3,2,1,0:T(8,128)S(1)}, f32[2,2,256,256]{3,2,1,0:T(8,128)}, u32[]{:S(2)}) copy-start(f32[2,2,256,256]{3,2,1,0:T(8,128)} %param.5) | copy-start | bytes 3145732
  6.5 233.4 %all-reduce.11.cloned.1.call-start = ((), (), s32[]{:S(2)}) async-start(), calls=%async_computation.2 | async-start | bytes 4194304 | tf_op jit(solution)/shard_map/psum | solution.py:101
  8.4 21.4 %collective-permute-start = (f32[2,128,384]{2,1,0:T(8,128)}, f32[2,128,384]{2,1,0:T(8,128)S(1)}, u32[]{:S(2)}, u32[]{:S(2)}) collective-permute-start(f32[2,128,384]{2,1,0:T(8,128)} %slice.359), channel_id=1, source_target_pairs={{4,0},{8,4},{12,8},{16,12},{20,16},{24,20},{28,24},{5,1},{9,5},{13... | collective-permute-start | bytes 1179656 | tf_op jit(solution)/shard_map/ppermute | solution.py:17
  53.7 72.2 %copy-start.1 = (f32[1,4,256,256]{3,2,1,0:T(8,128)S(1)}, f32[1,4,256,256]{3,2,1,0:T(8,128)}, u32[]{:S(2)}) copy-start(f32[1,4,256,256]{3,2,1,0:T(8,128)} %param.6) | copy-start | bytes 3145732
  53.7 24.8 %collective-permute-start.1 = (f32[4,256,256]{2,1,0:T(8,128)S(1)}, f32[4,256,256]{2,1,0:T(8,128)S(1)}, u32[]{:S(2)}, u32[]{:S(2)}) collective-permute-start(f32[4,256,256]{2,1,0:T(8,128)S(1)} %bitcast_reduce_fusion.2), channel_id=1, source_target_pairs={{0,1},{1,0},{2,3},{3,2},{4,5},{5,4},{6,7},{7,6},{8,9},{9,8},{10,11... | collective-permute-start | bytes 3145736 | tf_op jit(solution)/shard_map/ppermute | solution.py:87
  78.7 47.3 %collective-permute-start.2 = (f32[4,256,256]{2,1,0:T(8,128)S(1)}, f32[4,256,256]{2,1,0:T(8,128)S(1)}, u32[]{:S(2)}, u32[]{:S(2)}) collective-permute-start(f32[4,256,256]{2,1,0:T(8,128)S(1)} %add.313), channel_id=1, source_target_pairs={{0,2},{1,3},{2,0},{3,1},{4,6},{5,7},{6,4},{7,5},{8,10},{9,11},{10,... | collective-permute-start | bytes 3145736 | tf_op jit(solution)/shard_map/ppermute | solution.py:87
  151.6 364.4 %all-reduce.9.cloned.1.call-start = ((), (), s32[]{:S(2)}) async-start(), calls=%async_computation.1 | async-start | bytes 4194304 | tf_op jit(solution)/shard_map/psum | solution.py:101
  239.9 2.2 copy-start.7
  273.4 10.0 %collective-permute-start.3 = (f32[2,128,384]{2,1,0:T(8,128)S(1)}, f32[2,128,384]{2,1,0:T(8,128)S(1)}, u32[]{:S(2)}, u32[]{:S(2)}) collective-permute-start(f32[2,128,384]{2,1,0:T(8,128)S(1)} %slice.485), channel_id=1, source_target_pairs={{0,4},{4,8},{8,12},{12,16},{16,20},{20,24},{24,28},{1,5},{5,9},{9,... | collective-permute-start | bytes 1179656 | tf_op jit(solution)/shard_map/ppermute | solution.py:17
  283.5 0.7 copy-start.5
  299.6 8.6 %copy-start = (f32[2,256,384]{2,1,0:T(8,128)}, f32[2,256,384]{2,1,0:T(8,128)S(1)}, u32[]{:S(2)}) copy-start(f32[2,256,384]{2,1,0:T(8,128)S(1)} %multiply_add_fusion.8) | copy-start | bytes 2359300
  299.6 7.2 collective-permute-start.4
  331.4 74.4 %copy-start.2 = (f32[1,4,256,256]{3,2,1,0:T(8,128)S(1)}, f32[1,4,256,256]{3,2,1,0:T(8,128)}, u32[]{:S(2)}) copy-start(f32[1,4,256,256]{3,2,1,0:T(8,128)} %param.6) | copy-start | bytes 3145732
  331.4 25.3 %collective-permute-start.5 = (f32[4,256,256]{2,1,0:T(8,128)S(1)}, f32[4,256,256]{2,1,0:T(8,128)S(1)}, u32[]{:S(2)}, u32[]{:S(2)}) collective-permute-start(f32[4,256,256]{2,1,0:T(8,128)S(1)} %bitcast_reduce_fusion.1), channel_id=1, source_target_pairs={{0,1},{1,0},{2,3},{3,2},{4,5},{5,4},{6,7},{7,6},{8,9},{9,8},{10,11... | collective-permute-start | bytes 3145736 | tf_op jit(solution)/shard_map/ppermute | solution.py:87
  356.9 48.9 %collective-permute-start.6 = (f32[4,256,256]{2,1,0:T(8,128)S(1)}, f32[4,256,256]{2,1,0:T(8,128)S(1)}, u32[]{:S(2)}, u32[]{:S(2)}) collective-permute-start(f32[4,256,256]{2,1,0:T(8,128)S(1)} %add.331), channel_id=1, source_target_pairs={{0,2},{1,3},{2,0},{3,1},{4,6},{5,7},{6,4},{7,5},{8,10},{9,11},{10,... | collective-permute-start | bytes 3145736 | tf_op jit(solution)/shard_map/ppermute | solution.py:87
  431.4 360.1 %all-reduce.7.cloned.1.call-start = ((), (), s32[]{:S(2)}) async-start(), calls=%async_computation | async-start | bytes 4194304 | tf_op jit(solution)/shard_map/psum | solution.py:101
  516.0 2.2 copy-start.8
  549.5 10.0 %collective-permute-start.7 = (f32[2,128,384]{2,1,0:T(8,128)S(1)}, f32[2,128,384]{2,1,0:T(8,128)S(1)}, u32[]{:S(2)}, u32[]{:S(2)}) collective-permute-start(f32[2,128,384]{2,1,0:T(8,128)S(1)} %slice.515), channel_id=1, source_target_pairs={{0,4},{4,8},{8,12},{12,16},{16,20},{20,24},{24,28},{1,5},{5,9},{9,... | collective-permute-start | bytes 1179656 | tf_op jit(solution)/shard_map/ppermute | solution.py:17
  559.6 0.7 copy-start.4
  575.6 7.2 collective-permute-start.8
  607.1 74.4 %copy-start.3 = (f32[1,4,256,256]{3,2,1,0:T(8,128)S(1)}, f32[1,4,256,256]{3,2,1,0:T(8,128)}, u32[]{:S(2)}) copy-start(f32[1,4,256,256]{3,2,1,0:T(8,128)} %param.6) | copy-start | bytes 3145732
  607.1 25.3 %collective-permute-start.9 = (f32[4,256,256]{2,1,0:T(8,128)S(1)}, f32[4,256,256]{2,1,0:T(8,128)S(1)}, u32[]{:S(2)}, u32[]{:S(2)}) collective-permute-start(f32[4,256,256]{2,1,0:T(8,128)S(1)} %bitcast_reduce_fusion), channel_id=1, source_target_pairs={{0,1},{1,0},{2,3},{3,2},{4,5},{5,4},{6,7},{7,6},{8,9},{9,8},{10,11... | collective-permute-start | bytes 3145736 | tf_op jit(solution)/shard_map/ppermute | solution.py:87
  632.6 48.9 %collective-permute-start.10 = (f32[4,256,256]{2,1,0:T(8,128)S(1)}, f32[4,256,256]{2,1,0:T(8,128)S(1)}, u32[]{:S(2)}, u32[]{:S(2)}) collective-permute-start(f32[4,256,256]{2,1,0:T(8,128)S(1)} %add.349), channel_id=1, source_target_pairs={{0,2},{1,3},{2,0},{3,1},{4,6},{5,7},{6,4},{7,5},{8,10},{9,11},{10,... | collective-permute-start | bytes 3145736 | tf_op jit(solution)/shard_map/ppermute | solution.py:87
  791.5 2.1 copy-start.9
  824.0 10.0 %collective-permute-start.11 = (f32[2,128,384]{2,1,0:T(8,128)S(1)}, f32[2,128,384]{2,1,0:T(8,128)S(1)}, u32[]{:S(2)}, u32[]{:S(2)}) collective-permute-start(f32[2,128,384]{2,1,0:T(8,128)S(1)} %slice.545), channel_id=1, source_target_pairs={{0,4},{4,8},{8,12},{12,16},{16,20},{20,24},{24,28},{1,5},{5,9},{9,... | collective-permute-start | bytes 1179656 | tf_op jit(solution)/shard_map/ppermute | solution.py:17
Sparse Core Ops, SparseCore 0:
  151.7 88.1 all-reduce.10
  431.5 84.3 all-reduce.8
  707.1 84.3 all-reduce.6
